TPU v7x, 128 devices: a whole 4x4x4 slice. The times are simulated.
128 devices in a mesh: cfg: 2 (over core), lat: 4 (over x), seq: 16 (over z, y).
Axes of the slice: x: 4, y: 4, z: 4, core: 2. Of those that a mesh axis runs over, the one named last changes fastest.
Arguments:
- latents: float32 [24, 1024, 16], P('lat', 'seq'), may hold values from -6 to 6
- timesteps: int32 [24], P('lat'), may hold values from 0 to 999
- labels: int32 [24], P('lat'), may hold values from 0 to 999
- guidance: float32 [1], replicated, may hold values from 1.5 to 4
- keep_coef: float32 [24], P('lat'), may hold values from 0.8 to 1.2
- noise_coef: float32 [24], P('lat'), may hold values from -0.6 to -0.2
- w_patch: bfloat16 [16, 1152], replicated, may hold values from -1.5 to 1.5
- label_table: bfloat16 [1001, 1152], replicated, may hold values from -6 to 6
- w_time1: bfloat16 [256, 1152], P(None, 'lat'), may hold values from -0.375 to 0.375
- w_time2: bfloat16 [1152, 1152], P(None, 'lat'), may hold values from -0.1875 to 0.1875
- ada_weight: bfloat16 [1152, 9216], P(None, 'seq'), may hold values from -0.1875 to 0.1875
- w_qkv: bfloat16 [1152, 3456], P(None, 'seq'), may hold values from -2.9168155 to 2.9168155
- w_proj: bfloat16 [1152, 1152], P(None, 'seq'), may hold values from -0.1875 to 0.1875
- w_fc1: bfloat16 [1152, 4608], P(None, 'seq'), may hold values from -0.1875 to 0.1875
- w_fc2: bfloat16 [4608, 1152], P('seq'), may hold values from -0.09375 to 0.09375
- w_out: bfloat16 [1152, 16], replicated, may hold values from -0.1875 to 0.1875
Outputs:
- next_latents: float32 [24, 1024, 16], P('lat', 'seq', 'cfg')
All inputs are finite; a program needn't handle non-finite values.
Results may differ from a plain program's by a relative error of at most 0.009.
Values may be sent and summed in bfloat16 or wider, within the bound.
A program may use at most 192 MiB of HBM per device.

v0:
```python
import math
import jax
import jax.numpy as jnp
from jax import lax
from jax.sharding import PartitionSpec as P

D = 1152
HEADS = 16
HEAD_DIM = 72
CLASSES = 1000
FREQ = 256
GRID = 32


def swapped(value, axis, stride):
    mask = 2**stride
    pairs = [(source, source ^ mask) for source in range(lax.axis_size(axis))]
    return lax.ppermute(value, axis, pairs)


def layer_norm(values):
    average = jnp.mean(values, axis=-1, keepdims=True)
    centered = values - average
    spread = jnp.mean(centered * centered, axis=-1, keepdims=True)
    return centered * lax.rsqrt(spread + 1e-06)


def modulate(values, shifted, scaled):
    return layer_norm(values) * (1.0 + scaled[:, None, :]) + shifted[:, None, :]


def time_waves(timesteps):
    half_count = FREQ // 2
    frequency = jnp.exp(-math.log(10000.0) * jnp.arange(half_count, dtype=jnp.float32) / half_count)
    angles = timesteps.astype(jnp.float32)[:, None] * frequency[None, :]
    return jnp.concatenate([jnp.cos(angles), jnp.sin(angles)], axis=-1)


def grid_waves(positions):
    quarter = D // 4
    frequency = jnp.exp(-math.log(10000.0) * jnp.arange(quarter, dtype=jnp.float32) / quarter)
    column = (positions % GRID).astype(jnp.float32)[:, None] * frequency[None, :]
    row_angle = (positions // GRID).astype(jnp.float32)[:, None] * frequency[None, :]
    return jnp.concatenate(
        [jnp.sin(column), jnp.cos(column), jnp.sin(row_angle), jnp.cos(row_angle)], axis=-1
    )


def condition(timesteps, classes, label_table, w_time1, w_time2):
    waves = time_waves(timesteps).astype(jnp.bfloat16)
    hidden_time = jax.nn.silu(jnp.dot(waves, w_time1, preferred_element_type=jnp.float32)).astype(
        jnp.bfloat16
    )
    time_vector = jnp.dot(hidden_time, w_time2, preferred_element_type=jnp.float32)
    onehot = (classes[:, None] == jnp.arange(CLASSES + 1, dtype=jnp.int32)[None, :]).astype(
        jnp.bfloat16
    )
    return time_vector + jnp.dot(onehot, label_table, preferred_element_type=jnp.float32)


def shards(
    latents,
    timesteps,
    labels,
    guidance,
    keep_coef,
    noise_coef,
    w_patch,
    label_table,
    w_time1,
    w_time2,
    ada_weight,
    w_qkv,
    w_proj,
    w_fc1,
    w_fc2,
    w_out,
):
    lat_count, tok_count, channels = latents.shape
    model_width = w_patch.shape[1]
    side_index = lax.axis_index("cfg")
    classes = jnp.where(side_index == 0, labels, CLASSES)
    time_first, time_second = (
        lax.all_gather(w_time1, "lat", axis=1, tiled=True),
        lax.all_gather(w_time2, "lat", axis=1, tiled=True),
    )
    conditioning = condition(timesteps, classes, label_table, time_first, time_second)
    own_columns = jnp.dot(
        jax.nn.silu(conditioning).astype(jnp.bfloat16),
        ada_weight,
        preferred_element_type=jnp.float32,
    )
    modulation = lax.all_gather(own_columns, "seq", axis=1, tiled=True)
    pieces = [
        modulation[:, number * model_width : (number + 1) * model_width] for number in range(8)
    ]
    positions = lax.axis_index("seq") * tok_count + jnp.arange(tok_count, dtype=jnp.int32)
    state = jnp.dot(
        latents.reshape(-1, channels).astype(jnp.bfloat16),
        w_patch,
        preferred_element_type=jnp.float32,
    )
    state = state.reshape(lat_count, tok_count, model_width) + grid_waves(positions)[None]
    qkv_full, proj_full = (
        lax.all_gather(w_qkv, "seq", axis=1, tiled=True),
        lax.all_gather(w_proj, "seq", axis=1, tiled=True),
    )
    normed = modulate(state, pieces[0], pieces[1]).astype(jnp.bfloat16).reshape(-1, model_width)
    triple = jnp.dot(normed, qkv_full, preferred_element_type=jnp.float32).astype(jnp.bfloat16)
    queries = triple[:, :model_width].reshape(lat_count, tok_count, HEADS, HEAD_DIM)
    keys_own = triple[:, model_width : 2 * model_width].reshape(lat_count, tok_count, model_width)
    values_own = triple[:, 2 * model_width :].reshape(lat_count, tok_count, model_width)
    factor = 1.0 / math.sqrt(HEAD_DIM)
    row_best = jnp.full((lat_count, HEADS, tok_count), -1e30, jnp.float32)
    keys_part = lax.all_gather(keys_own, "seq", axis=1, tiled=True)
    values_part = lax.all_gather(values_own, "seq", axis=1, tiled=True)
    key_count = keys_part.shape[1]
    keys_heads = keys_part.reshape(lat_count, key_count, HEADS, HEAD_DIM)
    values_heads = values_part.reshape(lat_count, key_count, HEADS, HEAD_DIM)
    scores = (
        jnp.einsum("lqhd,lkhd->lhqk", queries, keys_heads, preferred_element_type=jnp.float32)
        * factor
    )
    raised = jnp.maximum(row_best, jnp.max(scores, axis=-1))
    exponent = jnp.exp(scores - raised[..., None])
    row_sums = jnp.sum(exponent, axis=-1)
    weighted = jnp.einsum(
        "lhqk,lkhd->lhqd",
        exponent.astype(jnp.bfloat16),
        values_heads,
        preferred_element_type=jnp.float32,
    )
    row_best, row_sums, weighted = (raised, row_sums, weighted)
    attended = (
        (weighted / row_sums[..., None])
        .transpose(0, 2, 1, 3)
        .reshape(-1, model_width)
        .astype(jnp.bfloat16)
    )
    projected = jnp.dot(attended, proj_full, preferred_element_type=jnp.float32)
    state = state + pieces[2][:, None, :] * projected.reshape(lat_count, tok_count, model_width)
    normed = modulate(state, pieces[3], pieces[4]).astype(jnp.bfloat16).reshape(-1, model_width)
    fc1_full, fc2_full = (
        lax.all_gather(w_fc1, "seq", axis=1, tiled=True),
        lax.all_gather(w_fc2, "seq", axis=0, tiled=True),
    )
    hidden = jax.nn.gelu(
        jnp.dot(normed, fc1_full, preferred_element_type=jnp.float32), approximate=True
    ).astype(jnp.bfloat16)
    mlp_out = jnp.dot(hidden, fc2_full, preferred_element_type=jnp.float32)
    state = state + pieces[5][:, None, :] * mlp_out.reshape(lat_count, tok_count, model_width)
    final = modulate(state, pieces[6], pieces[7]).astype(jnp.bfloat16).reshape(-1, model_width)
    noise_own = jnp.dot(final, w_out, preferred_element_type=jnp.float32).reshape(
        lat_count, tok_count, channels
    )
    half_width = channels // 2
    own_latent = lax.dynamic_slice_in_dim(latents, side_index * half_width, half_width, 2)
    partner = swapped(noise_own, "cfg", 0)
    cond_noise = jnp.where(side_index == 0, noise_own, partner)
    free_noise = jnp.where(side_index == 0, partner, noise_own)
    combined = free_noise + guidance[0] * (cond_noise - free_noise)
    guided = lax.dynamic_slice_in_dim(combined, side_index * half_width, half_width, 2)
    return keep_coef[:, None, None] * own_latent + noise_coef[:, None, None] * guided


def solution(mesh):
    return jax.shard_map(
        shards,
        mesh=mesh,
        in_specs=(
            P("lat", "seq", None),
            P("lat"),
            P("lat"),
            P(),
            P("lat"),
            P("lat"),
            P(),
            P(),
            P(None, "lat"),
            P(None, "lat"),
            P(None, "seq"),
            P(None, "seq"),
            P(None, "seq"),
            P(None, "seq"),
            P("seq", None),
            P(),
        ),
        out_specs=P("lat", "seq", "cfg"),
        check_vma=False,
    )
```

profile of v0, /device:TPU:1, one launch (start us, length us, event | category | flops | bytes accessed | tf_op | source)
XLA Modules:
  0.0 571.2 jit_solution(164010904563712114)
XLA Ops:
  6.5 0.0 copy-start
  6.5 0.0 all-gather.9.cloned.1.call-start
  6.5 0.7 all-gather.9.cloned.1.call-update
  7.3 0.0 all-gather.11.cloned.1.call-start
  7.3 0.7 all-gather.11.cloned.1.call-update
  8.0 0.0 all-gather.13.cloned.1.call-start
  8.1 0.7 convert_element_type.57
  8.7 0.8 multiply_cosine_fusion
  9.5 0.0 copy-start.5
  9.5 0.2 concatenate.7
  9.7 0.0 copy-done.6
  9.7 0.0 copy-start.10
  9.7 1.3 fusion.61
  11.0 0.0 copy-start.2
  11.0 1.2 copy-done.2
  12.2 0.3 multiply_reduce_fusion.3
  12.6 0.0 copy-done.5
  12.6 12.5 %all_gather.27 = bf16[256,1152]{0,1:T(8,128)(2,1)S(1)} all-gather(bf16[256,288]{0,1:T(8,128)(2,1)S(1)} %copy-done.5), channel_id=1, replica_groups=mesh['cfg'=2,'lat'=4,'seq'=16] {'lat'}, dimensions={1}, use_global_device_ids=true | all-gather | bytes 737280 | tf_op jit(solution)/shard_map/all_gather | solution.py:84
  25.0 0.0 copy-done.10
  25.1 0.1 fusion.36
  25.2 23.4 %all-gather.9.cloned.1.call-done = bf16[1152,1152]{0,1:T(8,128)(2,1)} async-done(((bf16[1152,288]{0,1:T(8,128)(2,1)}), bf16[1152,1152]{0,1:T(8,128)(2,1)}) %all-gather.9.cloned.1.call-update) | async-done | bytes 2654224 | tf_op jit(solution)/shard_map/all_gather | solution.py:85
  48.6 2.7 fusion.31
  51.3 0.0 copy-done
  51.3 2.1 convolution_bitcast_fusion
  53.5 21.0 %all-gather = f32[16,576,6]{1,2,0:T(8,128)S(1)} all-gather(f32[1,576,6]{1,2,0:T(8,128)S(1)} %convolution_bitcast_fusion), channel_id=1, replica_groups=mesh['cfg'=2,'lat'=4,'seq'=16] {'seq'}, dimensions={0}, use_global_device_ids=true | all-gather | bytes 235008 | tf_op jit(solution)/shard_map/all_gather | solution.py:93
  74.5 0.1 reshape.145
  74.7 0.0 copy-done.3
  74.7 0.5 add_convert_fusion.2
  75.1 45.3 %all-gather.11.cloned.1.call-done = bf16[1152,3456]{0,1:T(8,128)(2,1)} async-done(((bf16[1152,216]{0,1:T(8,128)(2,1)}), bf16[1152,3456]{0,1:T(8,128)(2,1)}) %all-gather.11.cloned.1.call-update) | async-done | bytes 7962640 | tf_op jit(solution)/shard_map/all_gather | solution.py:105
  120.4 8.3 %convolution_convert_fusion = bf16[384,3456]{1,0:T(8,128)(2,1)S(1)} fusion(bf16[384,1152]{1,0:T(8,128)(2,1)S(1)} %bitcast.55, bf16[1152,3456]{0,1:T(8,128)(2,1)} %all-gather.11.cloned.1.call-done), kind=kOutput, calls=%fused_computation.16 | convolution fusion | flops 3058974720 | bytes 11501568 | tf_op jit(solution)/shard_map/dot_general | solution.py:109
  128.7 1.5 fusion.60
  130.1 0.0 all-gather.13.cloned.1.call-update
  130.2 0.0 all-gather.15.cloned.1.call-start
  130.2 0.5 all-gather.15.cloned.1.call-update
  130.7 0.0 all-gather.17.cloned.1.call-start
  130.8 0.5 all-gather.17.cloned.1.call-update
  131.3 0.0 all-gather.19.cloned.1.call-start
  131.4 0.5 all-gather.19.cloned.1.call-update
  131.9 0.2 all-gather.21.cloned.1.call-start
  132.1 0.5 all-gather.21.cloned.1.call-update
  132.6 3.6 reshape.137
  136.3 91.6 %all-gather.13.cloned.1.call-done = bf16[6,1024,1152]{2,1,0:T(8,128)(2,1)} async-done(((bf16[6,64,1152]{2,1,0:T(8,128)(2,1)}), bf16[6,1024,1152]{2,1,0:T(8,128)(2,1)}) %all-gather.13.cloned.1.call-update) | async-done | bytes 14155792 | tf_op jit(solution)/shard_map/all_gather | solution.py:115
  227.9 18.7 %copy.27 = bf16[6,1024,1152]{1,2,0:T(8,128)(2,1)} copy(bf16[6,1024,1152]{2,1,0:T(8,128)(2,1)} %all-gather.13.cloned.1.call-done) | data formatting | bytes 28311552 | tf_op jit(solution)/shard_map/all_gather | solution.py:115
  246.7 80.9 %all-gather.15.cloned.1.call-done = bf16[6,1024,1152]{2,1,0:T(8,128)(2,1)} async-done(((bf16[6,64,1152]{2,1,0:T(8,128)(2,1)}), bf16[6,1024,1152]{2,1,0:T(8,128)(2,1)}) %all-gather.15.cloned.1.call-update) | async-done | bytes 14155792 | tf_op jit(solution)/shard_map/all_gather | solution.py:116
  327.6 18.7 %copy.29 = bf16[6,1024,1152]{1,2,0:T(8,128)(2,1)} copy(bf16[6,1024,1152]{2,1,0:T(8,128)(2,1)} %all-gather.15.cloned.1.call-done) | data formatting | bytes 28311552 | tf_op jit(solution)/shard_map/all_gather | solution.py:116
  346.3 18.5 %multiply_reduce_fusion = (f32[6,16,64]{2,1,0:T(8,128)S(1)}, f32[6,16,64,1024]{3,2,1,0:T(8,128)}) fusion(bf16[6,1024,16,72]{1,3,2,0:T(8,128)(2,1)} %bitcast.48, bf16[6,64,16,72]{3,2,1,0:T(8,128)(2,1)} %reshape.137), kind=kOutput, calls=%fused_computation.1 | convolution fusion | flops 918546432 | bytes 40230912 | tf_op jit(solution)/shard_map/lqhd,lkhd->lhqk/dot_general | solution.py:121
  364.8 11.2 %fusion = f32[6,16,64]{2,1,0:T(8,128)S(1)} fusion(f32[6,16,64,1024]{3,2,1,0:T(8,128)} %get-tuple-element.29, f32[6,16,64]{2,1,0:T(8,128)S(1)} %broadcast_maximum_fusion), kind=kLoop, calls=%fused_computation.2 | loop fusion | flops 18868224 | bytes 25214976 | tf_op jit(solution)/shard_map/reduce_sum | solution.py:126
  376.0 14.7 %fusion.20 = bf16[6,64,16,72]{3,1,2,0:T(8,128)(2,1)S(1)} fusion(bf16[6,1024,16,72]{1,3,2,0:T(8,128)(2,1)} %bitcast.49, f32[6,16,64,1024]{3,2,1,0:T(8,128)} %get-tuple-element.29, f32[6,16,64]{2,1,0:T(8,128)S(1)} %broadcast_maximum_fusion, f32[6,64,16]{1,2,0:T(8,128)S(1)} %bitcast.56), kind=kOutput, calls=%fused_computation.25 | convolution fusion | flops 925728768 | bytes 40255488 | tf_op jit(solution)/shard_map/lhqk,lkhd->lhqd/dot_general | solution.py:127
  390.8 2.2 copy.30
  393.0 3.2 convert_element_type.64
  396.2 0.0 all-gather.17.cloned.1.call-done
  396.2 3.3 fusion.62
  399.6 0.3 multiply_reduce_fusion.2
  400.0 0.9 copy-done.4
  400.9 0.4 add_convert_fusion.1
  401.3 56.8 %all-gather.19.cloned.1.call-done = bf16[1152,4608]{0,1:T(8,128)(2,1)} async-done(((bf16[1152,288]{0,1:T(8,128)(2,1)}), bf16[1152,4608]{0,1:T(8,128)(2,1)}) %all-gather.19.cloned.1.call-update) | async-done | bytes 10616848 | tf_op jit(solution)/shard_map/all_gather | solution.py:144
  458.1 82.9 %all-gather.21.cloned.1.call-done = bf16[4608,1152]{1,0:T(8,128)(2,1)} async-done(((bf16[288,1152]{1,0:T(8,128)(2,1)}), bf16[4608,1152]{1,0:T(8,128)(2,1)}) %all-gather.21.cloned.1.call-update) | async-done | bytes 10616848 | tf_op jit(solution)/shard_map/all_gather | solution.py:145
  540.9 17.6 %fusion.14 = f32[384,1152]{1,0:T(8,128)} fusion(bf16[4608,1152]{1,0:T(8,128)(2,1)} %all-gather.21.cloned.1.call-done, bf16[384,1152]{1,0:T(8,128)(2,1)S(1)} %bitcast.54, bf16[1152,4608]{0,1:T(8,128)(2,1)} %all-gather.19.cloned.1.call-done), kind=kOutput, calls=%fused_computation.17 | convolution fusion | flops 8169652224 | bytes 23887872 | tf_op jit(solution)/shard_map/dot_general | solution.py:150
  558.6 2.5 fusion.59
  561.1 0.3 multiply_reduce_fusion.1
  561.4 0.6 fusion.27
  562.0 0.7 collective-permute-start
  563.4 0.2 collective-permute-done
  563.6 0.7 multiply_add_fusion.1
  (24 shorter events, 0.2 us)
Async XLA Ops:
  6.5 44.8 %copy-start = (bf16[1001,1152]{1,0:T(8,128)(2,1)S(1)}, bf16[1001,1152]{1,0:T(8,128)(2,1)}, u32[]{:S(2)}) copy-start(bf16[1001,1152]{1,0:T(8,128)(2,1)} %param.23) | copy-start | bytes 6918916
  6.5 3.2 copy-start.6
  6.5 42.0 %all-gather.9.cloned.1.call-start = ((), (), s32[]{:S(2)}) async-start(), calls=%async_computation | async-start | bytes 3317760 | tf_op jit(solution)/shard_map/all_gather | solution.py:85
  7.3 113.1 %all-gather.11.cloned.1.call-start = ((), (), s32[]{:S(2)}) async-start(), calls=%async_computation.1 | async-start | bytes 8460288 | tf_op jit(solution)/shard_map/all_gather | solution.py:105
  8.0 219.9 %all-gather.13.cloned.1.call-start = ((), (), s32[]{:S(2)}) async-start(), calls=%async_computation.2 | async-start | bytes 15040512 | tf_op jit(solution)/shard_map/all_gather | solution.py:115
  9.5 3.0 copy-start.5
  9.7 15.3 %copy-start.10 = (s32[6]{0:T(128)S(1)}, s32[6]{0:T(128)}, u32[]{:S(2)}) copy-start(s32[6]{0:T(128)} %param.18) | copy-start | bytes 76
  11.0 1.2 copy-start.2
  53.5 21.2 %copy-start.3 = (f32[6,64,1152]{2,1,0:T(8,128)S(1)}, f32[6,64,1152]{2,1,0:T(8,128)}, u32[]{:S(2)}) copy-start(f32[6,64,1152]{2,1,0:T(8,128)} %copy-done.2) | copy-start | bytes 5308420
  130.2 197.4 %all-gather.15.cloned.1.call-start = ((), (), s32[]{:S(2)}) async-start(), calls=%async_computation.3 | async-start | bytes 15040512 | tf_op jit(solution)/shard_map/all_gather | solution.py:116
  130.7 265.5 %all-gather.17.cloned.1.call-start = ((), (), s32[]{:S(2)}) async-start(), calls=%async_computation.4 | async-start | bytes 2820096 | tf_op jit(solution)/shard_map/all_gather | solution.py:106
  131.3 326.7 %all-gather.19.cloned.1.call-start = ((), (), s32[]{:S(2)}) async-start(), calls=%async_computation.5 | async-start | bytes 11280384 | tf_op jit(solution)/shard_map/all_gather | solution.py:144
  131.9 409.0 %all-gather.21.cloned.1.call-start = ((), (), s32[]{:S(2)}) async-start(), calls=%async_computation.6 | async-start | bytes 11280384 | tf_op jit(solution)/shard_map/all_gather | solution.py:145
  399.6 1.3 copy-start.4
  558.6 2.9 copy-start.9
  558.6 5.7 %copy-start.1 = (bf16[1001,1152]{1,0:T(8,128)(2,1)S(1)}, bf16[1001,1152]{1,0:T(8,128)(2,1)}, u32[]{:S(2)}) copy-start(bf16[1001,1152]{1,0:T(8,128)(2,1)} %param.23) | copy-start | bytes 6918916
  561.1 2.5 copy-start.7
  561.1 2.5 copy-start.8
  562.0 1.6 collective-permute-start
Sparse Core Ops, SparseCore 0:
  9.0 39.5 all-gather.8
  50.7 69.6 all-gather.10
  130.3 97.5 all-gather.12
  229.9 97.6 all-gather.14
  329.6 45.8 all-gather.16
  377.4 80.5 all-gather.18
  460.2 80.6 all-gather.20
where the time goes:
time: 573 us; the launch traced here: 571 us
  waiting for transfers between devices  385 us (67%)
  matrix products  69.3 us (12%)
  local copies, waits for them, and re-layouts  50.5 us (9%)
  blocking collectives  33.4 us (6%)
  other arithmetic  17.8 us (3%)
  between operations  14.4 us (3%)
    all_gather x1, waiting for transfers between devices, shards(): keys_part = lax.all_gather(keys_own, 'seq', axis=1, tiled=True)  91.6 us
    all_gather x1, waiting for transfers between devices, shards(): lax.all_gather(w_fc2, 'seq', axis=0, tiled=True)  82.9 us
    all_gather x1, waiting for transfers between devices, shards(): values_part = lax.all_gather(values_own, 'seq', axis=1, tiled=True)  80.9 us
    all_gather x1, waiting for transfers between devices, shards(): lax.all_gather(w_fc1, 'seq', axis=1, tiled=True)  56.8 us
    all_gather x1, waiting for transfers between devices, shards(): lax.all_gather(w_qkv, 'seq', axis=1, tiled=True)  45.3 us
    all_gather x1, waiting for transfers between devices, shards(): lax.all_gather(w_time2, 'lat', axis=1, tiled=True)  23.4 us
    all_gather x1, blocking collectives, shards(): modulation = lax.all_gather(own_columns, 'seq', axis=1, tiled=True)  21 us
    all_gather x1, local copies, waits for them, and re-layouts, shards(): keys_part = lax.all_gather(keys_own, 'seq', axis=1, tiled=True)  18.7 us
  transfers between devices with their start and end apart: 8, of which 7 were waited for; matrix products, arithmetic and copies ran while one was open for 18% of the time, Pallas kernels for 0%

commit v1 on v0

--- a/solution.py
+++ b/solution.py
@@ -112,8 +112,11 @@
     values_own = triple[:, 2 * model_width :].reshape(lat_count, tok_count, model_width)
     factor = 1.0 / math.sqrt(HEAD_DIM)
     row_best = jnp.full((lat_count, HEADS, tok_count), -1e30, jnp.float32)
-    keys_part = lax.all_gather(keys_own, "seq", axis=1, tiled=True)
-    values_part = lax.all_gather(values_own, "seq", axis=1, tiled=True)
+    keys_part, values_part = jnp.split(
+        lax.all_gather(jnp.concatenate([keys_own, values_own], axis=0), "seq", tiled=True, axis=1),
+        [keys_own.shape[0]],
+        0,
+    )
     key_count = keys_part.shape[1]
     keys_heads = keys_part.reshape(lat_count, key_count, HEADS, HEAD_DIM)
     values_heads = values_part.reshape(lat_count, key_count, HEADS, HEAD_DIM)

time: 573 us -> 545 us (0.951)
  waiting for transfers between devices: 385 us -> 336 us
  local copies, waits for them, and re-layouts: 50.5 us -> 69.5 us
    split x0 -> x3, local copies, waits for them, and re-layouts: none -> 57.6 us  [shards(): jnp.split(lax.all_gather(jnp.concatenate([keys_own, values_own], axis=0),...]
    all_gather x1, waiting for transfers between devices: 56.8 us -> 16.7 us  [shards(): lax.all_gather(w_fc1, 'seq', axis=1, tiled=True)]
    all_gather x2 -> x0, local copies, waits for them, and re-layouts: 37.4 us -> none  [the longest x1 18.7 us: shards(): keys_part = lax.all_gather(keys_own, 'seq', axis=1, tiled=True)]
    all_gather x2 -> x1, waiting for transfers between devices: 173 us -> 165 us  [shards(): lax.all_gather(jnp.concatenate([keys_own, values_own], axis=0), 'seq', ti...]
  transfers between devices with their start and end apart: 8 -> 7, of which waited for: 7 -> 6; matrix products, arithmetic and copies ran while one was open for 18% -> 23% of each run, Pallas kernels for 0% -> 0%
where the time goes in v1:
time: 545 us; the launch traced here: 544 us
  waiting for transfers between devices  336 us (62%)
  matrix products  70.1 us (13%)
  local copies, waits for them, and re-layouts  69.5 us (13%)
  blocking collectives  33.5 us (6%)
  other arithmetic  19.6 us (4%)
  between operations  14.4 us (3%)
    all_gather x1, waiting for transfers between devices, shards(): lax.all_gather(jnp.concatenate([keys_own, values_own], axis=0), 'seq', ti...  165 us
    all_gather x1, waiting for transfers between devices, shards(): lax.all_gather(w_fc2, 'seq', axis=0, tiled=True)  82.7 us
    split x3, local copies, waits for them, and re-layouts, shards(): jnp.split(lax.all_gather(jnp.concatenate([keys_own, values_own], axis=0),...  57.6 us
    all_gather x1, waiting for transfers between devices, shards(): lax.all_gather(w_qkv, 'seq', axis=1, tiled=True)  45.3 us
    all_gather x1, waiting for transfers between devices, shards(): lax.all_gather(w_time2, 'lat', axis=1, tiled=True)  23.4 us
    all_gather x1, blocking collectives, shards(): modulation = lax.all_gather(own_columns, 'seq', axis=1, tiled=True)  21 us
    dot_general x1, matrix products, shards(): jnp.einsum('lqhd,lkhd->lhqk', queries, keys_heads, preferred_element_type...  19.1 us
    dot_general x1, matrix products, shards(): mlp_out = jnp.dot(hidden, fc2_full, preferred_element_type=jnp.float32)  17.6 us
  transfers between devices with their start and end apart: 7, of which 6 were waited for; matrix products, arithmetic and copies ran while one was open for 23% of the time, Pallas kernels for 0%

profile of v1, /device:TPU:1, one launch (start us, length us, event | category | flops | bytes accessed | tf_op | source)
XLA Modules:
  0.0 543.8 jit_solution(13782747618091548766)
XLA Ops:
  6.5 0.0 copy-start
  6.5 0.0 all-gather.8.cloned.1.call-start
  6.5 0.7 all-gather.8.cloned.1.call-update
  7.3 0.0 all-gather.10.cloned.1.call-start
  7.3 0.7 all-gather.10.cloned.1.call-update
  8.0 0.0 all-gather.12.cloned.1.call-start
  8.1 0.7 convert_element_type.57
  8.7 0.8 multiply_cosine_fusion
  9.5 0.0 copy-start.5
  9.5 0.2 concatenate.10
  9.7 0.0 copy-done.6
  9.7 0.0 copy-start.10
  9.7 1.3 fusion.62
  11.0 0.0 copy-start.2
  11.0 1.2 copy-done.2
  12.2 0.3 multiply_reduce_fusion.3
  12.5 0.0 copy-done.5
  12.5 12.5 %all_gather.24 = bf16[256,1152]{0,1:T(8,128)(2,1)S(1)} all-gather(bf16[256,288]{0,1:T(8,128)(2,1)S(1)} %copy-done.5), channel_id=1, replica_groups=mesh['cfg'=2,'lat'=4,'seq'=16] {'lat'}, dimensions={1}, use_global_device_ids=true | all-gather | bytes 737280 | tf_op jit(solution)/shard_map/all_gather | solution.py:84
  25.0 0.0 copy-done.10
  25.0 0.1 fusion.36
  25.2 23.4 %all-gather.8.cloned.1.call-done = bf16[1152,1152]{0,1:T(8,128)(2,1)} async-done(((bf16[1152,288]{0,1:T(8,128)(2,1)}), bf16[1152,1152]{0,1:T(8,128)(2,1)}) %all-gather.8.cloned.1.call-update) | async-done | bytes 2654224 | tf_op jit(solution)/shard_map/all_gather | solution.py:85
  48.6 2.7 fusion.31
  51.3 0.0 copy-done
  51.3 2.1 convolution_bitcast_fusion
  53.5 21.0 %all-gather = f32[16,576,6]{1,2,0:T(8,128)S(1)} all-gather(f32[1,576,6]{1,2,0:T(8,128)S(1)} %convolution_bitcast_fusion), channel_id=1, replica_groups=mesh['cfg'=2,'lat'=4,'seq'=16] {'seq'}, dimensions={0}, use_global_device_ids=true | all-gather | bytes 235008 | tf_op jit(solution)/shard_map/all_gather | solution.py:93
  74.5 0.1 reshape.145
  74.7 0.0 copy-done.3
  74.7 0.5 add_convert_fusion.2
  75.1 45.3 %all-gather.10.cloned.1.call-done = bf16[1152,3456]{0,1:T(8,128)(2,1)} async-done(((bf16[1152,216]{0,1:T(8,128)(2,1)}), bf16[1152,3456]{0,1:T(8,128)(2,1)}) %all-gather.10.cloned.1.call-update) | async-done | bytes 7962640 | tf_op jit(solution)/shard_map/all_gather | solution.py:105
  120.4 8.3 %convolution_convert_fusion = bf16[384,3456]{1,0:T(8,128)(2,1)S(1)} fusion(bf16[384,1152]{1,0:T(8,128)(2,1)S(1)} %bitcast.55, bf16[1152,3456]{0,1:T(8,128)(2,1)} %all-gather.10.cloned.1.call-done), kind=kOutput, calls=%fused_computation.16 | convolution fusion | flops 3058974720 | bytes 11501568 | tf_op jit(solution)/shard_map/dot_general | solution.py:109
  128.7 0.2 fusion.61
  128.9 1.4 pad_maximum_fusion
  130.3 0.0 all-gather.12.cloned.1.call-update
  130.3 0.0 all-gather.14.cloned.1.call-start
  130.3 0.5 all-gather.14.cloned.1.call-update
  130.9 0.0 all-gather.16.cloned.1.call-start
  130.9 0.5 all-gather.16.cloned.1.call-update
  131.5 0.2 all-gather.18.cloned.1.call-start
  131.7 0.3 all-gather.18.cloned.1.call-update
  132.0 3.7 reshape.137
  135.7 164.7 %all-gather.12.cloned.1.call-done = bf16[12,1024,1152]{2,1,0:T(8,128)(2,1)} async-done(((bf16[12,64,1152]{2,1,0:T(8,128)(2,1)}), bf16[12,1024,1152]{2,1,0:T(8,128)(2,1)}) %all-gather.12.cloned.1.call-update) | async-done | bytes 28311568 | tf_op jit(solution)/shard_map/all_gather | solution.py:116
  300.4 20.2 %fusion.60 = (bf16[6,1024,1152]{2,1,0:T(8,128)(2,1)}, bf16[6,1024,1152]{2,1,0:T(8,128)(2,1)}) fusion(bf16[12,1024,1152]{2,1,0:T(8,128)(2,1)} %all-gather.12.cloned.1.call-done), kind=kLoop, calls=%fused_computation.94 | loop fusion | bytes 56623104 | tf_op jit(solution)/shard_map/split | solution.py:115
  320.6 18.7 %copy.27 = bf16[6,1024,1152]{1,2,0:T(8,128)(2,1)} copy(bf16[6,1024,1152]{2,1,0:T(8,128)(2,1)} %get-tuple-element.7) | data formatting | bytes 28311552 | tf_op jit(solution)/shard_map/split | solution.py:115
  339.3 18.7 %copy.29 = bf16[6,1024,1152]{1,2,0:T(8,128)(2,1)} copy(bf16[6,1024,1152]{2,1,0:T(8,128)(2,1)} %get-tuple-element.8) | data formatting | bytes 28311552 | tf_op jit(solution)/shard_map/split | solution.py:115
  358.0 19.1 %multiply_reduce_fusion = (f32[6,16,64]{2,1,0:T(8,128)S(1)}, f32[6,16,64,1024]{3,2,1,0:T(8,128)}) fusion(bf16[6,1024,16,72]{1,3,2,0:T(8,128)(2,1)} %bitcast.48, bf16[6,64,16,72]{3,2,1,0:T(8,128)(2,1)} %reshape.137), kind=kOutput, calls=%fused_computation.1 | convolution fusion | flops 918546432 | bytes 40230912 | tf_op jit(solution)/shard_map/lqhd,lkhd->lhqk/dot_general | solution.py:124
  377.1 11.6 %fusion = f32[6,16,64]{2,1,0:T(8,128)S(1)} fusion(f32[6,16,64,1024]{3,2,1,0:T(8,128)} %get-tuple-element.31, f32[6,16,64]{2,1,0:T(8,128)S(1)} %broadcast_maximum_fusion), kind=kLoop, calls=%fused_computation.2 | loop fusion | flops 18868224 | bytes 25214976 | tf_op jit(solution)/shard_map/reduce_sum | solution.py:129
  388.7 14.9 %fusion.20 = bf16[6,64,16,72]{3,1,2,0:T(8,128)(2,1)S(1)} fusion(bf16[6,1024,16,72]{1,3,2,0:T(8,128)(2,1)} %bitcast.49, f32[6,16,64,1024]{3,2,1,0:T(8,128)} %get-tuple-element.31, f32[6,16,64]{2,1,0:T(8,128)S(1)} %broadcast_maximum_fusion, f32[6,64,16]{1,2,0:T(8,128)S(1)} %bitcast.56), kind=kOutput, calls=%fused_computation.25 | convolution fusion | flops 925728768 | bytes 40255488 | tf_op jit(solution)/shard_map/lhqk,lkhd->lhqd/dot_general | solution.py:130
  403.6 2.3 copy.30
  405.9 3.2 convert_element_type.64
  409.1 0.0 all-gather.14.cloned.1.call-done
  409.2 3.4 fusion.63
  412.6 0.3 multiply_reduce_fusion.2
  412.9 0.9 copy-done.4
  413.8 0.4 add_convert_fusion.1
  414.2 16.7 %all-gather.16.cloned.1.call-done = bf16[1152,4608]{0,1:T(8,128)(2,1)} async-done(((bf16[1152,288]{0,1:T(8,128)(2,1)}), bf16[1152,4608]{0,1:T(8,128)(2,1)}) %all-gather.16.cloned.1.call-update) | async-done | bytes 10616848 | tf_op jit(solution)/shard_map/all_gather | solution.py:147
  430.9 82.7 %all-gather.18.cloned.1.call-done = bf16[4608,1152]{1,0:T(8,128)(2,1)} async-done(((bf16[288,1152]{1,0:T(8,128)(2,1)}), bf16[4608,1152]{1,0:T(8,128)(2,1)}) %all-gather.18.cloned.1.call-update) | async-done | bytes 10616848 | tf_op jit(solution)/shard_map/all_gather | solution.py:148
  513.6 17.6 %fusion.14 = f32[384,1152]{1,0:T(8,128)} fusion(bf16[4608,1152]{1,0:T(8,128)(2,1)} %all-gather.18.cloned.1.call-done, bf16[384,1152]{1,0:T(8,128)(2,1)S(1)} %bitcast.54, bf16[1152,4608]{0,1:T(8,128)(2,1)} %all-gather.16.cloned.1.call-done), kind=kOutput, calls=%fused_computation.17 | convolution fusion | flops 8169652224 | bytes 23887872 | tf_op jit(solution)/shard_map/dot_general | solution.py:153
  531.3 2.5 fusion.59
  533.8 0.3 multiply_reduce_fusion.1
  534.1 0.6 fusion.27
  534.7 0.7 collective-permute-start
  536.1 0.2 collective-permute-done
  536.3 0.0 copy-done.7
  536.3 0.7 multiply_add_fusion.1
  (23 shorter events, 0.2 us)
Async XLA Ops:
  6.5 44.8 %copy-start = (bf16[1001,1152]{1,0:T(8,128)(2,1)S(1)}, bf16[1001,1152]{1,0:T(8,128)(2,1)}, u32[]{:S(2)}) copy-start(bf16[1001,1152]{1,0:T(8,128)(2,1)} %param.23) | copy-start | bytes 6918916
  6.5 3.2 copy-start.6
  6.5 42.0 %all-gather.8.cloned.1.call-start = ((), (), s32[]{:S(2)}) async-start(), calls=%async_computation | async-start | bytes 3317760 | tf_op jit(solution)/shard_map/all_gather | solution.py:85
  7.3 113.1 %all-gather.10.cloned.1.call-start = ((), (), s32[]{:S(2)}) async-start(), calls=%async_computation.1 | async-start | bytes 8460288 | tf_op jit(solution)/shard_map/all_gather | solution.py:105
  8.0 292.4 %all-gather.12.cloned.1.call-start = ((), (), s32[]{:S(2)}) async-start(), calls=%async_computation.2 | async-start | bytes 30081024 | tf_op jit(solution)/shard_map/all_gather | solution.py:116
  9.5 3.0 copy-start.5
  9.7 15.3 %copy-start.10 = (s32[6]{0:T(128)S(1)}, s32[6]{0:T(128)}, u32[]{:S(2)}) copy-start(s32[6]{0:T(128)} %param.18) | copy-start | bytes 76
  11.0 1.2 copy-start.2
  53.5 21.2 %copy-start.3 = (f32[6,64,1152]{2,1,0:T(8,128)S(1)}, f32[6,64,1152]{2,1,0:T(8,128)}, u32[]{:S(2)}) copy-start(f32[6,64,1152]{2,1,0:T(8,128)} %copy-done.2) | copy-start | bytes 5308420
  130.3 278.9 %all-gather.14.cloned.1.call-start = ((), (), s32[]{:S(2)}) async-start(), calls=%async_computation.3 | async-start | bytes 2820096 | tf_op jit(solution)/shard_map/all_gather | solution.py:106
  130.9 300.0 %all-gather.16.cloned.1.call-start = ((), (), s32[]{:S(2)}) async-start(), calls=%async_computation.4 | async-start | bytes 11280384 | tf_op jit(solution)/shard_map/all_gather | solution.py:147
  131.5 382.2 %all-gather.18.cloned.1.call-start = ((), (), s32[]{:S(2)}) async-start(), calls=%async_computation.5 | async-start | bytes 11280384 | tf_op jit(solution)/shard_map/all_gather | solution.py:148
  412.6 1.2 copy-start.4
  531.2 2.9 copy-start.9
  531.3 5.7 %copy-start.1 = (bf16[1001,1152]{1,0:T(8,128)(2,1)S(1)}, bf16[1001,1152]{1,0:T(8,128)(2,1)}, u32[]{:S(2)}) copy-start(bf16[1001,1152]{1,0:T(8,128)(2,1)} %param.23) | copy-start | bytes 6918916
  533.8 2.5 copy-start.7
  533.8 2.5 copy-start.8
  534.7 1.6 collective-permute-start
Sparse Core Ops, SparseCore 0:
  9.0 39.5 all-gather.7
  50.7 69.6 all-gather.9
  130.4 169.9 all-gather.11
  302.4 45.8 all-gather.13
  350.3 80.5 all-gather.15
  432.9 80.6 all-gather.17
